TPU v7x, 128 devices: a whole 4x4x4 slice. The times are simulated.
128 devices in a mesh: gx: 16 (over x, z_hi, core), gy: 8 (over z_lo, y).
Axes of the slice: x: 4, y: 4, z: 4 (z_hi: 2, z_lo: 2; z = z_hi * 2 + z_lo), core: 2. Of those that a mesh axis runs over, the one named last changes fastest.
Arguments:
- volume: bfloat16 [64, 32, 128, 128], P(None, 'gx', 'gy'), may hold values from -6 to 6
- kernel: bfloat16 [4, 4, 4, 32, 64], replicated, may hold values from -0.25 to 0.25
- cotangent: bfloat16 [2, 2, 2, 32, 32, 128, 128], P(None, None, None, None, 'gx', 'gy'), may hold values from -6 to 6
Outputs:
- activation: bfloat16 [2, 2, 2, 32, 32, 128, 128], P(None, None, None, None, 'gx', 'gy')
- input_grad: bfloat16 [64, 32, 128, 128], P(None, 'gx', 'gy')
- weight_grad: float32 [4, 4, 4, 32, 64], replicated
All inputs are finite; a program needn't handle non-finite values.
Results may differ from a plain program's by a relative error of at most 0.0049.
Values may be sent and summed in bfloat16 or wider, within the bound.
A program may use at most 192 MiB of HBM per device.

v0:
```python
import math
import jax
import jax.numpy as jnp
from jax import lax
from jax.sharding import PartitionSpec as P

FORWARD_TAPS = (((1, 0), (3, -1)), ((2, 0), (0, 1)))
PHASE_TAPS = (((1, 0), (3, 1)), ((0, -1), (2, 0)))


def padded_2(block, sides, width):
    for axis, dim in sides:
        count = lax.axis_size(axis)
        forward = [(i, i + 1) for i in range(count - 1)]
        backward = [(target, source) for source, target in forward]
        low = lax.ppermute(
            lax.slice_in_dim(block, block.shape[dim] - width, None, axis=dim), axis, forward
        )
        high = lax.ppermute(lax.slice_in_dim(block, 0, width, axis=dim), axis, backward)
        block = jnp.concatenate([low, block, high], axis=dim)
    return block


def silu_pair(before):
    sigmoid = jax.nn.sigmoid(before)
    return (before * sigmoid, sigmoid * (1.0 + before * (1.0 - sigmoid)))


def phase_product(padded, kernel, phase_x, phase_y, phase_z, span_x, span_y, depth_cells):
    total = None
    for tap_x, shift_x in FORWARD_TAPS[phase_x]:
        for tap_y, shift_y in FORWARD_TAPS[phase_y]:
            for tap_z, shift_z in FORWARD_TAPS[phase_z]:
                piece = lax.slice(
                    padded,
                    (0, 1 + shift_x, 1 + shift_y, 1 + shift_z),
                    (
                        padded.shape[0],
                        1 + shift_x + span_x,
                        1 + shift_y + span_y,
                        1 + shift_z + depth_cells,
                    ),
                )
                term = lax.dot_general(
                    kernel[tap_x, tap_y, tap_z],
                    piece,
                    (((1,), (0,)), ((), ())),
                    preferred_element_type=jnp.float32,
                )
                total = term if total is None else total + term
    return total


def all_phases(padded, kernel, span_x, span_y, depth_cells):
    results = []
    for phase_x in range(2):
        for phase_y in range(2):
            for phase_z in range(2):
                results.append(
                    phase_product(
                        padded, kernel, phase_x, phase_y, phase_z, span_x, span_y, depth_cells
                    )
                )
    chans_out = results[0].shape[0]
    return jnp.stack(results).reshape(2, 2, 2, chans_out, span_x, span_y, depth_cells)


def on_device(volume, kernel, cotangent):
    cells_x = volume.shape[1]
    cells_y = volume.shape[2]
    depth_cells = volume.shape[3]
    rim_cells = padded_2(volume, (("gx", 1), ("gy", 2)), 1)
    padded = jnp.pad(rim_cells, ((0, 0), (0, 0), (0, 0), (1, 1)))
    before = all_phases(padded, kernel, cells_x, cells_y, depth_cells)
    values, slopes = silu_pair(before)
    activation = values.astype(jnp.bfloat16)
    grad_pre = (cotangent.astype(jnp.float32) * slopes).astype(jnp.bfloat16)
    grad_rim = padded_2(grad_pre, (("gx", 4), ("gy", 5)), 1)
    grad_pad = jnp.pad(grad_rim, ((0, 0), (0, 0), (0, 0), (0, 0), (0, 0), (0, 0), (1, 1)))
    chans_out = grad_pad.shape[3]
    back_sum = None
    weight_parts = [None] * 64
    for phase_x in range(2):
        for phase_y in range(2):
            for phase_z in range(2):
                source = grad_pad[phase_x, phase_y, phase_z]
                group_list = []
                group_slots = []
                for tap_x, shift_x in PHASE_TAPS[phase_x]:
                    for tap_y, shift_y in PHASE_TAPS[phase_y]:
                        for tap_z, shift_z in PHASE_TAPS[phase_z]:
                            piece = lax.slice(
                                source,
                                (0, 1 + shift_x, 1 + shift_y, 1 + shift_z),
                                (
                                    chans_out,
                                    1 + shift_x + cells_x,
                                    1 + shift_y + cells_y,
                                    1 + shift_z + depth_cells,
                                ),
                            )
                            product = lax.dot_general(
                                kernel[tap_x, tap_y, tap_z],
                                piece,
                                (((0,), (0,)), ((), ())),
                                preferred_element_type=jnp.float32,
                            )
                            back_sum = product if back_sum is None else back_sum + product
                            group_list.append(
                                lax.dot_general(
                                    piece,
                                    volume,
                                    (((1, 2, 3), (1, 2, 3)), ((), ())),
                                    preferred_element_type=jnp.float32,
                                )
                            )
                            group_slots.append(16 * tap_x + 4 * tap_y + tap_z)
                group_terms = jnp.stack(group_list)
                for position, flat_index in enumerate(group_slots):
                    weight_parts[flat_index] = group_terms[position]
    input_grad = back_sum.astype(jnp.bfloat16)
    stacked_grad = jnp.stack(weight_parts).reshape(4, 4, 4, chans_out, volume.shape[0])
    stacked_grad = lax.psum(stacked_grad, ("gx", "gy"))
    scaling = 1.0 / math.sqrt(
        cells_x * lax.axis_size("gx") * cells_y * lax.axis_size("gy") * depth_cells
    )
    return (activation, input_grad, stacked_grad * scaling)


def solution(mesh):
    placed = (P(None, "gx", "gy", None), P(), P(None, None, None, None, "gx", "gy", None))
    return jax.shard_map(
        on_device,
        mesh=mesh,
        in_specs=placed,
        out_specs=(P(None, None, None, None, "gx", "gy", None), P(None, "gx", "gy", None), P()),
        check_vma=False,
    )
```

profile of v0, /device:TPU:1, one launch (start us, length us, event | category | flops | bytes accessed | tf_op | source)
XLA Modules:
  0.0 342.6 jit_solution(13506336892047364948)
XLA Ops:
  8.6 6.9 %collective-permute-start = (bf16[64,1,16,128]{3,0,2,1:T(8,128)(2,1)S(1)}, bf16[64,1,16,128]{3,0,2,1:T(8,128)(2,1)S(1)}, u32[]{:S(2)}, u32[]{:S(2)}) collective-permute-start(bf16[64,1,16,128]{3,0,2,1:T(8,128)(2,1)S(1)} %get-tuple-element.25), channel_id=1, source_target_pairs={{0,8},{8,16},{16,24},{24,32},{32,40},{40,48},{48,56},{56,64},{64,7... | collective-permute-start | bytes 786440 | tf_op jit(solution)/shard_map/ppermute | solution.py:16
  15.5 1.9 collective-permute-start.1
  20.0 4.7 %collective-permute-done.1 = bf16[64,1,16,128]{3,0,2,1:T(8,128)(2,1)S(1)} collective-permute-done((bf16[64,1,16,128]{3,0,2,1:T(8,128)(2,1)S(1)}, bf16[64,1,16,128]{3,0,2,1:T(8,128)(2,1)S(1)}, u32[]{:S(2)}, u32[]{:S(2)}) %collective-permute-start.1) | collective-permute-done | bytes 262176 | tf_op jit(solution)/shard_map/ppermute | solution.py:19
  24.7 3.2 collective-permute-start.2
  31.0 2.0 collective-permute-done.3
  33.0 1.8 fusion.11
  49.2 2.5 multiply_convert_fusion
  52.1 3.4 collective-permute-start.4
  55.5 1.9 collective-permute-start.5
  57.4 23.8 %collective-permute-done.4 = bf16[2,2,2,32,1,16,128]{6,3,5,4,2,1,0:T(8,128)(2,1)S(1)} collective-permute-done((bf16[2,2,2,32,1,16,128]{6,3,5,4,2,1,0:T(8,128)(2,1)S(1)}, bf16[2,2,2,32,1,16,128]{6,3,5,4,2,1,0:T(8,128)(2,1)S(1)}, u32[]{:S(2)}, u32[]{:S(2)}) %collective-permute-start.4) | collective-permute-done | bytes 1048608 | tf_op jit(solution)/shard_map/ppermute | solution.py:16
  83.9 2.1 copy.84
  86.1 3.7 %collective-permute-done.7 = bf16[2,2,2,32,4,1,128]{6,3,5,4,2,1,0:T(8,128)(2,1)S(1)} collective-permute-done((bf16[2,2,2,32,4,1,128]{6,3,5,4,2,1,0:T(8,128)(2,1)S(1)}, bf16[2,2,2,32,4,1,128]{6,3,5,4,2,1,0:T(8,128)(2,1)S(1)}, u32[]{:S(2)}, u32[]{:S(2)}) %collective-permute-start.7) | collective-permute-done | bytes 262176 | tf_op jit(solution)/shard_map/ppermute | solution.py:19
  89.8 8.8 %select_maximum_fusion = bf16[2,2,2,32,4,18,130]{6,3,5,4,2,1,0:T(8,128)(2,1)S(1)} fusion(bf16[2,2,2,32,4,1,128]{6,3,5,4,2,1,0:T(8,128)(2,1)S(1)} %collective-permute-done.7, bf16[2,2,2,32,4,1,128]{6,3,5,4,2,1,0:T(8,128)(2,1)S(1)} %collective-permute-done.6, bf16[2,2,2,32,1,16,128]{6,3,5,4,2,1,0:T(8,128)(2,1)S(1)} %collective-permute-done.5, ...), kind=kLoop, calls=%fused_computation.3 | loop fusion | flops 43130880 | bytes 9510912 | tf_op jit(solution)/shard_map/concatenate | solution.py:20
  99.8 1.7 convolution_bitcast_fusion.40
  101.6 1.8 convolution_bitcast_fusion.41
  151.0 1.5 convolution_bitcast_fusion.2
  180.1 1.9 convolution_add_fusion.15
  188.2 1.8 fusion.54
  190.5 1.9 fusion.59
  193.9 1.9 fusion.58
  197.2 1.9 fusion.57
  200.4 1.9 fusion.56
  208.4 124.8 %all-reduce.4.cloned.1.call-done = f32[4,4,4,32,64]{4,3,2,1,0:T(8,128)} async-done(((f32[4,4,4,32,64]{4,3,2,1,0:T(8,128)}), f32[4,4,4,32,64]{4,3,2,1,0:T(8,128)}) %all-reduce.4.cloned.1.call-update) | async-done | bytes 524304 | tf_op jit(solution)/shard_map/psum | solution.py:123
  333.2 2.3 broadcast_multiply_fusion
  (309 shorter events, 117.2 us)
Async XLA Ops:
  7.2 10.3 %copy-start = (bf16[64,2,16,128]{3,2,1,0:T(8,128)(2,1)S(1)}, bf16[64,2,16,128]{3,2,1,0:T(8,128)(2,1)}, u32[]{:S(2)}) copy-start(bf16[64,2,16,128]{3,2,1,0:T(8,128)(2,1)} %param.3) | copy-start | bytes 1572868
  7.2 10.3 %copy-start.51 = (bf16[4,4,4,32,64]{4,3,2,1,0:T(8,128)(2,1)S(1)}, bf16[4,4,4,32,64]{4,3,2,1,0:T(8,128)(2,1)}, u32[]{:S(2)}) copy-start(bf16[4,4,4,32,64]{4,3,2,1,0:T(8,128)(2,1)} %param.4) | copy-start | bytes 786436
  7.2 326.0 %all-reduce.4.cloned.1.call-start = ((), (), s32[]{:S(2)}) async-start(), calls=%async_computation | async-start | bytes 2097152 | tf_op jit(solution)/shard_map/psum | solution.py:123
  8.6 11.1 %collective-permute-start = (bf16[64,1,16,128]{3,0,2,1:T(8,128)(2,1)S(1)}, bf16[64,1,16,128]{3,0,2,1:T(8,128)(2,1)S(1)}, u32[]{:S(2)}, u32[]{:S(2)}) collective-permute-start(bf16[64,1,16,128]{3,0,2,1:T(8,128)(2,1)S(1)} %get-tuple-element.25), channel_id=1, source_target_pairs={{0,8},{8,16},{16,24},{24,32},{32,40},{40,48},{48,56},{56,64},{64,7... | collective-permute-start | bytes 786440 | tf_op jit(solution)/shard_map/ppermute | solution.py:16
  15.5 9.2 %collective-permute-start.1 = (bf16[64,1,16,128]{3,0,2,1:T(8,128)(2,1)S(1)}, bf16[64,1,16,128]{3,0,2,1:T(8,128)(2,1)S(1)}, u32[]{:S(2)}, u32[]{:S(2)}) collective-permute-start(bf16[64,1,16,128]{3,0,2,1:T(8,128)(2,1)S(1)} %get-tuple-element.24), channel_id=1, source_target_pairs={{8,0},{16,8},{24,16},{32,24},{40,32},{48,40},{56,48},{64,56},{72,6... | collective-permute-start | bytes 786440 | tf_op jit(solution)/shard_map/ppermute | solution.py:19
  24.7 6.2 %collective-permute-start.2 = (bf16[64,4,1,128]{3,0,2,1:T(8,128)(2,1)S(1)}, bf16[64,4,1,128]{3,0,2,1:T(8,128)(2,1)S(1)}, u32[]{:S(2)}, u32[]{:S(2)}) collective-permute-start(bf16[64,4,1,128]{3,0,2,1:T(8,128)(2,1)S(1)} %get-tuple-element.22), channel_id=1, source_target_pairs={{0,1},{1,2},{2,3},{3,4},{4,5},{5,6},{6,7},{8,9},{9,10},{10,11},{11... | collective-permute-start | bytes 196616 | tf_op jit(solution)/shard_map/ppermute | solution.py:16
  28.0 5.0 %collective-permute-start.3 = (bf16[64,4,1,128]{3,0,2,1:T(8,128)(2,1)S(1)}, bf16[64,4,1,128]{3,0,2,1:T(8,128)(2,1)S(1)}, u32[]{:S(2)}, u32[]{:S(2)}) collective-permute-start(bf16[64,4,1,128]{3,0,2,1:T(8,128)(2,1)S(1)} %get-tuple-element.23), channel_id=1, source_target_pairs={{1,0},{2,1},{3,2},{4,3},{5,4},{6,5},{7,6},{9,8},{10,9},{11,10},{12... | collective-permute-start | bytes 196616 | tf_op jit(solution)/shard_map/ppermute | solution.py:19
  52.1 29.1 %collective-permute-start.4 = (bf16[2,2,2,32,1,16,128]{6,3,5,4,2,1,0:T(8,128)(2,1)S(1)}, bf16[2,2,2,32,1,16,128]{6,3,5,4,2,1,0:T(8,128)(2,1)S(1)}, u32[]{:S(2)}, u32[]{:S(2)}) collective-permute-start(bf16[2,2,2,32,1,16,128]{6,3,5,4,2,1,0:T(8,128)(2,1)S(1)} %get-tuple-element.18), channel_id=1, source_target_pairs={{0,8},{8,16},{16,24},{24,32},{32,40},{40,48},{48,56},{56,64},{64,7... | collective-permute-start | bytes 3145736 | tf_op jit(solution)/shard_map/ppermute | solution.py:16
  55.5 25.8 %collective-permute-start.5 = (bf16[2,2,2,32,1,16,128]{6,3,5,4,2,1,0:T(8,128)(2,1)S(1)}, bf16[2,2,2,32,1,16,128]{6,3,5,4,2,1,0:T(8,128)(2,1)S(1)}, u32[]{:S(2)}, u32[]{:S(2)}) collective-permute-start(bf16[2,2,2,32,1,16,128]{6,3,5,4,2,1,0:T(8,128)(2,1)S(1)} %get-tuple-element.19), channel_id=1, source_target_pairs={{8,0},{16,8},{24,16},{32,24},{40,32},{48,40},{56,48},{64,56},{72,6... | collective-permute-start | bytes 3145736 | tf_op jit(solution)/shard_map/ppermute | solution.py:19
  81.3 4.8 %collective-permute-start.6 = (bf16[2,2,2,32,4,1,128]{6,3,5,4,2,1,0:T(8,128)(2,1)S(1)}, bf16[2,2,2,32,4,1,128]{6,3,5,4,2,1,0:T(8,128)(2,1)S(1)}, u32[]{:S(2)}, u32[]{:S(2)}) collective-permute-start(bf16[2,2,2,32,4,1,128]{6,3,5,4,2,1,0:T(8,128)(2,1)S(1)} %get-tuple-element.14), channel_id=1, source_target_pairs={{0,1},{1,2},{2,3},{3,4},{4,5},{5,6},{6,7},{8,9},{9,10},{10,11},{11... | collective-permute-start | bytes 786440 | tf_op jit(solution)/shard_map/ppermute | solution.py:16
  82.6 7.1 %collective-permute-start.7 = (bf16[2,2,2,32,4,1,128]{6,3,5,4,2,1,0:T(8,128)(2,1)S(1)}, bf16[2,2,2,32,4,1,128]{6,3,5,4,2,1,0:T(8,128)(2,1)S(1)}, u32[]{:S(2)}, u32[]{:S(2)}) collective-permute-start(bf16[2,2,2,32,4,1,128]{6,3,5,4,2,1,0:T(8,128)(2,1)S(1)} %get-tuple-element.15), channel_id=1, source_target_pairs={{1,0},{2,1},{3,2},{4,3},{5,4},{6,5},{7,6},{9,8},{10,9},{11,10},{12... | collective-permute-start | bytes 786440 | tf_op jit(solution)/shard_map/ppermute | solution.py:19
  99.8 73.0 %copy-start.1 = (bf16[32,4,18,130]{3,0,2,1:T(8,128)(2,1)}, bf16[32,4,18,130]{3,0,2,1:T(8,128)(2,1)S(1)}, u32[]{:S(2)}) copy-start(bf16[32,4,18,130]{3,0,2,1:T(8,128)(2,1)S(1)} %get-tuple-element.8) | copy-start | bytes 1797124
  99.8 73.3 %copy-start.2 = (bf16[32,4,18,130]{3,0,2,1:T(8,128)(2,1)}, bf16[32,4,18,130]{3,0,2,1:T(8,128)(2,1)S(1)}, u32[]{:S(2)}) copy-start(bf16[32,4,18,130]{3,0,2,1:T(8,128)(2,1)S(1)} %get-tuple-element.9) | copy-start | bytes 1797124
  99.8 77.2 %copy-start.3 = (bf16[32,4,18,130]{3,0,2,1:T(8,128)(2,1)}, bf16[32,4,18,130]{3,0,2,1:T(8,128)(2,1)S(1)}, u32[]{:S(2)}) copy-start(bf16[32,4,18,130]{3,0,2,1:T(8,128)(2,1)S(1)} %get-tuple-element.10) | copy-start | bytes 1797124
  99.8 77.6 %copy-start.4 = (bf16[32,4,18,130]{3,0,2,1:T(8,128)(2,1)}, bf16[32,4,18,130]{3,0,2,1:T(8,128)(2,1)S(1)}, u32[]{:S(2)}) copy-start(bf16[32,4,18,130]{3,0,2,1:T(8,128)(2,1)S(1)} %get-tuple-element.11) | copy-start | bytes 1797124
  99.8 78.6 %copy-start.5 = (bf16[32,4,18,130]{3,0,2,1:T(8,128)(2,1)}, bf16[32,4,18,130]{3,0,2,1:T(8,128)(2,1)S(1)}, u32[]{:S(2)}) copy-start(bf16[32,4,18,130]{3,0,2,1:T(8,128)(2,1)S(1)} %get-tuple-element.6) | copy-start | bytes 1797124
  99.8 78.9 %copy-start.7 = (bf16[32,4,18,130]{3,0,2,1:T(8,128)(2,1)}, bf16[32,4,18,130]{3,0,2,1:T(8,128)(2,1)S(1)}, u32[]{:S(2)}) copy-start(bf16[32,4,18,130]{3,0,2,1:T(8,128)(2,1)S(1)} %get-tuple-element.12) | copy-start | bytes 1797124
  187.0 3.0 copy-start.49
  190.5 3.0 copy-start.41
  190.5 3.3 copy-start.42
  193.9 3.2 copy-start.35
  197.1 3.3 copy-start.28
  200.4 3.0 copy-start.20
  200.4 3.3 copy-start.21
  (38 other events, 81.7 us)
Sparse Core Ops, SparseCore 0:
  180.2 152.9 all-reduce.3
where the time goes:
time: 346 us; the launch traced here: 343 us
  waiting for transfers between devices  159 us (46%)
  matrix products  114 us (33%)
  starting transfers between devices  21.2 us (6%)
  local copies, waits for them, and re-layouts  17.6 us (5%)
  other arithmetic  15.5 us (4%)
  between operations  15.3 us (4%)
    psum x1, waiting for transfers between devices, on_device(): stacked_grad = lax.psum(stacked_grad, ('gx', 'gy'))  125 us
    dot_general x64, matrix products, on_device(): lax.dot_general(kernel[tap_x, tap_y, tap_z], piece, (((0,), (0,)), ((), (...  75.5 us
    ppermute x4, waiting for transfers between devices, padded_2(): lax.ppermute(lax.slice_in_dim(block, block.shape[dim] - width, None, axis...  23.8 us
    dot_general x64, matrix products, on_device(): lax.dot_general(piece, volume, (((1, 2, 3), (1, 2, 3)), ((), ())), prefer...  21.3 us
    dot_general x64, matrix products, phase_product(): lax.dot_general(kernel[tap_x, tap_y, tap_z], piece, (((1,), (0,)), ((), (...  17 us
    unnamed x111, local copies, waits for them, and re-layouts  15.9 us
    ppermute x4, starting transfers between devices, padded_2(): lax.ppermute(lax.slice_in_dim(block, block.shape[dim] - width, None, axis...  14.8 us
    concatenate x3, other arithmetic, padded_2(): block = jnp.concatenate([low, block, high], axis=dim)  10.7 us
  transfers between devices with their start and end apart: 9, of which 5 were waited for; matrix products, arithmetic and copies ran while one was open for 7% of the time, Pallas kernels for 0%

commit v1 on v0

--- a/solution.py
+++ b/solution.py
@@ -120,7 +120,7 @@
                     weight_parts[flat_index] = group_terms[position]
     input_grad = back_sum.astype(jnp.bfloat16)
     stacked_grad = jnp.stack(weight_parts).reshape(4, 4, 4, chans_out, volume.shape[0])
-    stacked_grad = lax.psum(stacked_grad, ("gx", "gy"))
+    stacked_grad = lax.psum(lax.psum(stacked_grad, "gx"), "gy")
     scaling = 1.0 / math.sqrt(
         cells_x * lax.axis_size("gx") * cells_y * lax.axis_size("gy") * depth_cells
     )

time: 346 us -> 417 us (1.21)
  the two profiles are of different devices: /device:TPU:1 before, /device:TPU:0 now
where the time goes in v1:
time: 417 us; the launch traced here: 413 us
  waiting for transfers between devices  230 us (55%)
  matrix products  117 us (28%)
  starting transfers between devices  20.3 us (5%)
  other arithmetic  15.5 us (4%)
  local copies, waits for them, and re-layouts  15.3 us (4%)
  between operations  15.3 us (4%)
    psum x2, waiting for transfers between devices, on_device(): stacked_grad = lax.psum(lax.psum(stacked_grad, 'gx'), 'gy')  214 us
    dot_general x64, matrix products, on_device(): lax.dot_general(kernel[tap_x, tap_y, tap_z], piece, (((0,), (0,)), ((), (...  77.8 us
    dot_general x64, matrix products, on_device(): lax.dot_general(piece, volume, (((1, 2, 3), (1, 2, 3)), ((), ())), prefer...  21.3 us
    dot_general x64, matrix products, phase_product(): lax.dot_general(kernel[tap_x, tap_y, tap_z], piece, (((1,), (0,)), ((), (...  17.5 us
    ppermute x4, starting transfers between devices, padded_2(): lax.ppermute(lax.slice_in_dim(block, block.shape[dim] - width, None, axis...  15.1 us
    ppermute x4, waiting for transfers between devices, padded_2(): lax.ppermute(lax.slice_in_dim(block, 0, width, axis=dim), axis, backward)  14.5 us
    unnamed x103, local copies, waits for them, and re-layouts  13.6 us
    concatenate x3, other arithmetic, padded_2(): block = jnp.concatenate([low, block, high], axis=dim)  10.7 us
  transfers between devices with their start and end apart: 10, of which 8 were waited for; matrix products, arithmetic and copies ran while one was open for 7% of the time, Pallas kernels for 0%

profile of v1, /device:TPU:0, one launch (start us, length us, event | category | flops | bytes accessed | tf_op | source)
XLA Modules:
  0.0 413.3 jit_solution(13001926286987998922)
XLA Ops:
  13.8 3.8 collective-permute-done.1
  17.6 3.5 collective-permute-start.2
  24.1 3.1 collective-permute-done.3
  27.3 1.8 fusion.11
  43.9 2.5 multiply_convert_fusion
  46.8 6.8 %collective-permute-start.4 = (bf16[2,2,2,32,1,16,128]{6,3,5,4,2,1,0:T(8,128)(2,1)S(1)}, bf16[2,2,2,32,1,16,128]{6,3,5,4,2,1,0:T(8,128)(2,1)S(1)}, u32[]{:S(2)}, u32[]{:S(2)}) collective-permute-start(bf16[2,2,2,32,1,16,128]{6,3,5,4,2,1,0:T(8,128)(2,1)S(1)} %get-tuple-element.18), channel_id=1, source_target_pairs={{0,8},{8,16},{16,24},{24,32},{32,40},{40,48},{48,56},{56,64},{64,7... | collective-permute-start | bytes 3145736 | tf_op jit(solution)/shard_map/ppermute | solution.py:16
  55.8 3.3 collective-permute-done.5
  59.1 3.5 collective-permute-start.6
  64.0 2.1 copy.84
  66.5 4.4 %collective-permute-done.7 = bf16[2,2,2,32,4,1,128]{6,3,5,4,2,1,0:T(8,128)(2,1)S(1)} collective-permute-done((bf16[2,2,2,32,4,1,128]{6,3,5,4,2,1,0:T(8,128)(2,1)S(1)}, bf16[2,2,2,32,4,1,128]{6,3,5,4,2,1,0:T(8,128)(2,1)S(1)}, u32[]{:S(2)}, u32[]{:S(2)}) %collective-permute-start.7) | collective-permute-done | bytes 262176 | tf_op jit(solution)/shard_map/ppermute | solution.py:19
  70.9 8.8 %select_maximum_fusion = bf16[2,2,2,32,4,18,130]{6,3,5,4,2,1,0:T(8,128)(2,1)S(1)} fusion(bf16[2,2,2,32,4,1,128]{6,3,5,4,2,1,0:T(8,128)(2,1)S(1)} %collective-permute-done.7, bf16[2,2,2,32,4,1,128]{6,3,5,4,2,1,0:T(8,128)(2,1)S(1)} %collective-permute-done.6, bf16[2,2,2,32,1,16,128]{6,3,5,4,2,1,0:T(8,128)(2,1)S(1)} %collective-permute-done.5, ...), kind=kLoop, calls=%fused_computation.3 | loop fusion | flops 43130880 | bytes 9510912 | tf_op jit(solution)/shard_map/concatenate | solution.py:20
  81.0 1.7 convolution_bitcast_fusion.40
  82.7 1.7 convolution_bitcast_fusion.41
  158.7 1.9 convolution_add_fusion.15
  166.8 1.8 fusion.54
  169.1 1.9 fusion.59
  172.4 1.9 fusion.58
  175.7 1.9 fusion.57
  178.9 1.9 fusion.56
  182.4 1.7 fusion.55
  184.1 139.0 %all-reduce.5.cloned.1.call-done = f32[4,4,4,32,64]{4,3,2,1,0:T(8,128)} async-done(((f32[4,4,4,32,64]{4,3,2,1,0:T(8,128)}), f32[4,4,4,32,64]{4,3,2,1,0:T(8,128)}) %all-reduce.5.cloned.1.call-update) | async-done | bytes 524304 | tf_op jit(solution)/shard_map/psum | solution.py:123
  324.6 2.9 fusion.60
  328.6 75.3 %all-reduce.7.cloned.1.call-done = f32[4,4,4,32,64]{4,3,2,1,0:T(8,128)} async-done(((f32[4,4,4,32,64]{4,3,2,1,0:T(8,128)}), f32[4,4,4,32,64]{4,3,2,1,0:T(8,128)}) %all-reduce.7.cloned.1.call-update) | async-done | bytes 524304 | tf_op jit(solution)/shard_map/psum | solution.py:123
  403.9 2.3 broadcast_multiply_fusion
  (304 shorter events, 118.7 us)
Async XLA Ops:
  7.2 4.1 copy-start
  7.2 4.1 copy-start.47
  7.2 315.9 %all-reduce.5.cloned.1.call-start = ((), (), s32[]{:S(2)}) async-start(), calls=%async_computation | async-start | bytes 2097152 | tf_op jit(solution)/shard_map/psum | solution.py:123
  8.6 4.9 %collective-permute-start = (bf16[64,1,16,128]{3,0,2,1:T(8,128)(2,1)S(1)}, bf16[64,1,16,128]{3,0,2,1:T(8,128)(2,1)S(1)}, u32[]{:S(2)}, u32[]{:S(2)}) collective-permute-start(bf16[64,1,16,128]{3,0,2,1:T(8,128)(2,1)S(1)} %get-tuple-element.25), channel_id=1, source_target_pairs={{0,8},{8,16},{16,24},{24,32},{32,40},{40,48},{48,56},{56,64},{64,7... | collective-permute-start | bytes 786440 | tf_op jit(solution)/shard_map/ppermute | solution.py:16
  9.9 7.6 %collective-permute-start.1 = (bf16[64,1,16,128]{3,0,2,1:T(8,128)(2,1)S(1)}, bf16[64,1,16,128]{3,0,2,1:T(8,128)(2,1)S(1)}, u32[]{:S(2)}, u32[]{:S(2)}) collective-permute-start(bf16[64,1,16,128]{3,0,2,1:T(8,128)(2,1)S(1)} %get-tuple-element.24), channel_id=1, source_target_pairs={{8,0},{16,8},{24,16},{32,24},{40,32},{48,40},{56,48},{64,56},{72,6... | collective-permute-start | bytes 786440 | tf_op jit(solution)/shard_map/ppermute | solution.py:19
  17.6 6.5 %collective-permute-start.2 = (bf16[64,4,1,128]{3,0,2,1:T(8,128)(2,1)S(1)}, bf16[64,4,1,128]{3,0,2,1:T(8,128)(2,1)S(1)}, u32[]{:S(2)}, u32[]{:S(2)}) collective-permute-start(bf16[64,4,1,128]{3,0,2,1:T(8,128)(2,1)S(1)} %get-tuple-element.22), channel_id=1, source_target_pairs={{0,1},{1,2},{2,3},{3,4},{4,5},{5,6},{6,7},{8,9},{9,10},{10,11},{11... | collective-permute-start | bytes 196616 | tf_op jit(solution)/shard_map/ppermute | solution.py:16
  21.1 6.2 %collective-permute-start.3 = (bf16[64,4,1,128]{3,0,2,1:T(8,128)(2,1)S(1)}, bf16[64,4,1,128]{3,0,2,1:T(8,128)(2,1)S(1)}, u32[]{:S(2)}, u32[]{:S(2)}) collective-permute-start(bf16[64,4,1,128]{3,0,2,1:T(8,128)(2,1)S(1)} %get-tuple-element.23), channel_id=1, source_target_pairs={{1,0},{2,1},{3,2},{4,3},{5,4},{6,5},{7,6},{9,8},{10,9},{11,10},{12... | collective-permute-start | bytes 196616 | tf_op jit(solution)/shard_map/ppermute | solution.py:19
  46.8 9.0 %collective-permute-start.4 = (bf16[2,2,2,32,1,16,128]{6,3,5,4,2,1,0:T(8,128)(2,1)S(1)}, bf16[2,2,2,32,1,16,128]{6,3,5,4,2,1,0:T(8,128)(2,1)S(1)}, u32[]{:S(2)}, u32[]{:S(2)}) collective-permute-start(bf16[2,2,2,32,1,16,128]{6,3,5,4,2,1,0:T(8,128)(2,1)S(1)} %get-tuple-element.18), channel_id=1, source_target_pairs={{0,8},{8,16},{16,24},{24,32},{32,40},{40,48},{48,56},{56,64},{64,7... | collective-permute-start | bytes 3145736 | tf_op jit(solution)/shard_map/ppermute | solution.py:16
  53.6 5.5 %collective-permute-start.5 = (bf16[2,2,2,32,1,16,128]{6,3,5,4,2,1,0:T(8,128)(2,1)S(1)}, bf16[2,2,2,32,1,16,128]{6,3,5,4,2,1,0:T(8,128)(2,1)S(1)}, u32[]{:S(2)}, u32[]{:S(2)}) collective-permute-start(bf16[2,2,2,32,1,16,128]{6,3,5,4,2,1,0:T(8,128)(2,1)S(1)} %get-tuple-element.19), channel_id=1, source_target_pairs={{8,0},{16,8},{24,16},{32,24},{40,32},{48,40},{56,48},{64,56},{72,6... | collective-permute-start | bytes 3145736 | tf_op jit(solution)/shard_map/ppermute | solution.py:19
  59.1 7.4 %collective-permute-start.6 = (bf16[2,2,2,32,4,1,128]{6,3,5,4,2,1,0:T(8,128)(2,1)S(1)}, bf16[2,2,2,32,4,1,128]{6,3,5,4,2,1,0:T(8,128)(2,1)S(1)}, u32[]{:S(2)}, u32[]{:S(2)}) collective-permute-start(bf16[2,2,2,32,4,1,128]{6,3,5,4,2,1,0:T(8,128)(2,1)S(1)} %get-tuple-element.14), channel_id=1, source_target_pairs={{0,1},{1,2},{2,3},{3,4},{4,5},{5,6},{6,7},{8,9},{9,10},{10,11},{11... | collective-permute-start | bytes 786440 | tf_op jit(solution)/shard_map/ppermute | solution.py:16
  62.7 8.3 %collective-permute-start.7 = (bf16[2,2,2,32,4,1,128]{6,3,5,4,2,1,0:T(8,128)(2,1)S(1)}, bf16[2,2,2,32,4,1,128]{6,3,5,4,2,1,0:T(8,128)(2,1)S(1)}, u32[]{:S(2)}, u32[]{:S(2)}) collective-permute-start(bf16[2,2,2,32,4,1,128]{6,3,5,4,2,1,0:T(8,128)(2,1)S(1)} %get-tuple-element.15), channel_id=1, source_target_pairs={{1,0},{2,1},{3,2},{4,3},{5,4},{6,5},{7,6},{9,8},{10,9},{11,10},{12... | collective-permute-start | bytes 786440 | tf_op jit(solution)/shard_map/ppermute | solution.py:19
  80.9 70.4 %copy-start.1 = (bf16[32,4,18,130]{3,0,2,1:T(8,128)(2,1)}, bf16[32,4,18,130]{3,0,2,1:T(8,128)(2,1)S(1)}, u32[]{:S(2)}) copy-start(bf16[32,4,18,130]{3,0,2,1:T(8,128)(2,1)S(1)} %get-tuple-element.8) | copy-start | bytes 1797124
  80.9 70.7 %copy-start.2 = (bf16[32,4,18,130]{3,0,2,1:T(8,128)(2,1)}, bf16[32,4,18,130]{3,0,2,1:T(8,128)(2,1)S(1)}, u32[]{:S(2)}) copy-start(bf16[32,4,18,130]{3,0,2,1:T(8,128)(2,1)S(1)} %get-tuple-element.9) | copy-start | bytes 1797124
  80.9 74.6 %copy-start.3 = (bf16[32,4,18,130]{3,0,2,1:T(8,128)(2,1)}, bf16[32,4,18,130]{3,0,2,1:T(8,128)(2,1)S(1)}, u32[]{:S(2)}) copy-start(bf16[32,4,18,130]{3,0,2,1:T(8,128)(2,1)S(1)} %get-tuple-element.10) | copy-start | bytes 1797124
  81.0 75.0 %copy-start.4 = (bf16[32,4,18,130]{3,0,2,1:T(8,128)(2,1)}, bf16[32,4,18,130]{3,0,2,1:T(8,128)(2,1)S(1)}, u32[]{:S(2)}) copy-start(bf16[32,4,18,130]{3,0,2,1:T(8,128)(2,1)S(1)} %get-tuple-element.11) | copy-start | bytes 1797124
  81.0 75.9 %copy-start.5 = (bf16[32,4,18,130]{3,0,2,1:T(8,128)(2,1)}, bf16[32,4,18,130]{3,0,2,1:T(8,128)(2,1)S(1)}, u32[]{:S(2)}) copy-start(bf16[32,4,18,130]{3,0,2,1:T(8,128)(2,1)S(1)} %get-tuple-element.6) | copy-start | bytes 1797124
  81.0 76.3 %copy-start.7 = (bf16[32,4,18,130]{3,0,2,1:T(8,128)(2,1)}, bf16[32,4,18,130]{3,0,2,1:T(8,128)(2,1)S(1)}, u32[]{:S(2)}) copy-start(bf16[32,4,18,130]{3,0,2,1:T(8,128)(2,1)S(1)} %get-tuple-element.12) | copy-start | bytes 1797124
  158.6 245.3 %all-reduce.7.cloned.1.call-start = ((), (), s32[]{:S(2)}) async-start(), calls=%async_computation.1 | async-start | bytes 2097152 | tf_op jit(solution)/shard_map/psum | solution.py:123
  178.9 3.3 copy-start.12
  178.9 3.3 copy-start.13
  178.9 3.3 copy-start.14
  178.9 3.3 copy-start.15
  178.9 3.3 copy-start.16
  178.9 3.3 copy-start.17
  (35 other events, 78.4 us)
Sparse Core Ops, SparseCore 0:
  158.8 164.2 all-reduce.4
  325.6 78.3 all-reduce.6
